TPU v7x, 32 devices: a whole 2x2x4 slice. The times are simulated.
32 devices in a mesh: seq: 8 (over y, x, core), head: 4 (over z).
Axes of the slice: x: 2, y: 2, z: 4, core: 2. Of those that a mesh axis runs over, the one named last changes fastest.
Arguments:
- queries: bfloat16 [2, 8, 8, 32, 128], P(None, 'head'), may hold values from -128 to 128
- tree_keys: bfloat16 [2, 8, 32, 128], P(None, 'head'), may hold values from -8 to 8
- tree_values: bfloat16 [2, 8, 32, 128], P(None, 'head'), may hold values from -6 to 6
- cache_keys: bfloat16 [8, 8192, 128], P('head', 'seq'), may hold values from -6 to 6
- cache_values: bfloat16 [8, 8192, 128], P('head', 'seq'), may hold values from -6 to 6
- block_ids: int32 [8, 32], P('head'), may hold values from 0 to 63, as said below
- ancestors: int32 [1, 32, 32], replicated, may hold values from 0 to 1, as said below
- out_weight: bfloat16 [8192, 8192], P('seq', 'head'), may hold values from -0.0625 to 0.0625
Outputs:
- draft_mixed: bfloat16 [32, 1, 8192], P('seq', None, 'head')
- verify_mixed: bfloat16 [32, 1, 8192], P('seq', None, 'head')
Inputs may be any that keep to these rules, and one draw needn't show every extreme that they name: `block_ids`: the 32 block numbers of one pair are distinct, and for every pair one run of 1024 positions (positions s * 1024 to (s + 1) * 1024 - 1 for some s) holds at least half of its 32 blocks, or all 8 blocks of the run where the run has fewer. ancestors[r, n, k] is 1 exactly when k is n or an ancestor of n in request r's tree; node 0 is the root and every other node's parent has a smaller number.
All inputs are finite; a program needn't handle non-finite values.
Results may differ from a plain program's by a relative error of at most 0.009.
Values may be sent and summed in bfloat16 or wider, within the bound.
A program may use at most 64 MiB of HBM per device.

v0:
```python
import jax
import jax.numpy as jnp
from jax import lax
from jax.sharding import PartitionSpec as P

KVH = 8
BLOCK = 128


def cache_partial(query_rows, key_rows, value_rows, chosen_mask, score_scale):
    scores = (
        jnp.einsum("pgnh,plh->pgnl", query_rows, key_rows, preferred_element_type=jnp.float32)
        * score_scale
    )
    if chosen_mask is not None:
        scores = jnp.where(chosen_mask[:, None, None, :], scores, -1e30)
    peaks = jnp.max(scores, axis=-1)
    weights = jnp.exp(scores - peaks[..., None])
    if chosen_mask is not None:
        weights = jnp.where(chosen_mask[:, None, None, :], weights, 0.0)
    totals = jnp.sum(weights, axis=-1)
    summed = jnp.einsum(
        "pgnl,plh->pgnh",
        weights.astype(jnp.bfloat16),
        value_rows,
        preferred_element_type=jnp.float32,
    )
    return (peaks, totals, summed)


def tree_partial(query_rows, tree_key_rows, tree_value_rows, tree_mask, score_scale):
    scores = (
        jnp.einsum("pgnh,pkh->pgnk", query_rows, tree_key_rows, preferred_element_type=jnp.float32)
        * score_scale
    )
    allowed = tree_mask[:, None] > 0
    scores = jnp.where(allowed, scores, -1e30)
    peaks = jnp.max(scores, axis=-1)
    weights = jnp.where(allowed, jnp.exp(scores - peaks[..., None]), 0.0)
    totals = jnp.sum(weights, axis=-1)
    summed = jnp.einsum(
        "pgnk,pkh->pgnh",
        weights.astype(jnp.bfloat16),
        tree_value_rows,
        preferred_element_type=jnp.float32,
    )
    return (peaks, totals, summed)


def combine_two(first_part, second_part):
    peaks = jnp.maximum(first_part[0], second_part[0])
    first_factor = jnp.exp(first_part[0] - peaks)
    second_factor = jnp.exp(second_part[0] - peaks)
    totals = first_part[1] * first_factor + second_part[1] * second_factor
    summed = first_part[2] * first_factor[..., None] + second_part[2] * second_factor[..., None]
    return (peaks, totals, summed)


def combine_over(peaks, totals, summed):
    highest = jnp.max(peaks, axis=0)
    factor = jnp.exp(peaks - highest[None])
    return (highest, jnp.sum(totals * factor, axis=0), jnp.sum(summed * factor[..., None], axis=0))


def finish(cache_part, tree_part):
    peaks, totals, summed = combine_two(cache_part, tree_part)
    result = summed / totals[..., None]
    pair_count, groups, node_count, head_dim = result.shape
    return (
        jnp.transpose(result, (0, 2, 1, 3))
        .reshape(pair_count, node_count, groups * head_dim)
        .astype(jnp.bfloat16)
    )


def local(
    queries, tree_keys, tree_values, cache_keys, cache_values, block_ids, ancestors, out_weight
):
    pair_dev, ctx_dev, head_dim = cache_keys.shape
    groups = queries.shape[2]
    node_count = queries.shape[3]
    requests = ancestors.shape[0]
    score_scale = head_dim ** (-0.5)
    seq_count = lax.axis_size("seq")
    seq_index = lax.axis_index("seq")
    head_index = lax.axis_index("head")
    blocks_dev = ctx_dev // BLOCK
    node_dev = node_count // seq_count
    pair_ids = head_index * pair_dev + jnp.arange(pair_dev, dtype=jnp.int32)
    picker = (pair_ids[:, None] // KVH == jnp.arange(requests, dtype=jnp.int32)[None, :]).astype(
        jnp.int32
    )
    tree_masks = jnp.sum(picker[:, :, None, None] * ancestors[None], axis=1)
    verify_part = cache_partial(queries[1], cache_keys, cache_values, None, score_scale)
    owned_ids = seq_index * blocks_dev + jnp.arange(blocks_dev, dtype=jnp.int32)
    chosen = jnp.any(block_ids[:, :, None] == owned_ids[None, None, :], axis=1)
    chosen_mask = jnp.broadcast_to(chosen[:, :, None], (pair_dev, blocks_dev, BLOCK)).reshape(
        pair_dev, ctx_dev
    )
    draft_part = cache_partial(queries[0], cache_keys, cache_values, chosen_mask, score_scale)
    arrived = (
        lax.all_to_all(draft_part[0][None], "seq", split_axis=3, concat_axis=0, tiled=True),
        lax.all_to_all(draft_part[1][None], "seq", split_axis=3, concat_axis=0, tiled=True),
        lax.all_to_all(draft_part[2][None], "seq", split_axis=3, concat_axis=0, tiled=True),
        lax.all_to_all(verify_part[0][None], "seq", split_axis=3, concat_axis=0, tiled=True),
        lax.all_to_all(verify_part[1][None], "seq", split_axis=3, concat_axis=0, tiled=True),
        lax.all_to_all(verify_part[2][None], "seq", split_axis=3, concat_axis=0, tiled=True),
    )
    draft_cache = combine_over(arrived[0], arrived[1], arrived[2])
    verify_cache = combine_over(arrived[3], arrived[4], arrived[5])
    row_start = seq_index * node_dev
    mask_rows = lax.dynamic_slice_in_dim(tree_masks, row_start, node_dev, 1)
    draft_tree = tree_partial(
        lax.dynamic_slice_in_dim(queries[0], row_start, node_dev, 2),
        tree_keys[0],
        tree_values[0],
        mask_rows,
        score_scale,
    )
    verify_tree = tree_partial(
        lax.dynamic_slice_in_dim(queries[1], row_start, node_dev, 2),
        tree_keys[1],
        tree_values[1],
        mask_rows,
        score_scale,
    )
    draft_all, verify_all = (
        lax.all_gather(finish(draft_cache, draft_tree), "seq", axis=1, tiled=True),
        lax.all_gather(finish(verify_cache, verify_tree), "seq", axis=1, tiled=True),
    )
    gathered = (
        lax.all_gather(draft_all, "head", axis=0, tiled=True),
        lax.all_gather(verify_all, "head", axis=0, tiled=True),
    )
    stacked = jnp.stack(gathered)
    stacked = stacked.reshape(2, requests, KVH, node_count, groups * head_dim)
    stacked = jnp.transpose(stacked, (3, 0, 1, 2, 4)).reshape(
        node_count, 2 * requests, KVH * groups * head_dim
    )
    rows_dev = out_weight.shape[0]
    columns = lax.dynamic_slice_in_dim(stacked, seq_index * rows_dev, rows_dev, 2)
    own_rows = lax.psum_scatter(
        jnp.einsum("nrk,kd->nrd", columns, out_weight, preferred_element_type=jnp.float32),
        "seq",
        scatter_dimension=0,
        tiled=True,
    )
    own_rows = own_rows.reshape(node_dev, 2, requests, own_rows.shape[-1]).astype(jnp.bfloat16)
    return (own_rows[:, 0], own_rows[:, 1])


def solution(mesh):
    in_specs = (
        P(None, "head", None, None, None),
        P(None, "head", None, None),
        P(None, "head", None, None),
        P("head", "seq", None),
        P("head", "seq", None),
        P("head", None),
        P(),
        P("seq", "head"),
    )
    out_specs = (P("seq", None, "head"), P("seq", None, "head"))
    return jax.shard_map(local, mesh=mesh, in_specs=in_specs, out_specs=out_specs, check_vma=False)
```

profile of v0, /device:TPU:0, one launch (start us, length us, event | category | flops | bytes accessed | tf_op | source)
XLA Modules:
  0.0 145.6 jit_solution(11215316324020661436)
XLA Ops:
  0.7 0.9 compare_reduce_fusion
  1.7 1.5 %fusion.2 = (f32[2,8,32]{2,1,0:T(8,128)S(1)}, f32[2,8,32,1024]{3,2,1,0:T(8,128)S(1)}) fusion(pred[2,1024]{1,0:T(4,128)(4,1)S(1)} %bitcast.216, bf16[2,1024,128]{2,1,0:T(8,128)(2,1)S(1)} %copy-done, bf16[2,2,8,32,128]{4,3,2,1,0:T(8,128)(2,1)} %param.8), kind=kOutput, calls=%fused_computation.6 | convolution fusion | flops 135790080 | bytes 2756608 | tf_op jit(solution)/shard_map/pgnh,plh->pgnl/dot_general | solution.py:12
  3.2 1.3 copy-done.1
  4.5 0.6 fusion.5
  5.2 0.7 copy.50
  5.9 5.2 %all-to-all-start.2 = ((f32[1,2,8,32]{2,1,0,3:T(2,128)}), f32[1,2,8,32]{2,1,0,3:T(2,128)}, u32[]{:S(2)}, u32[]{:S(2)}) async-start(f32[1,2,8,32]{2,1,0,3:T(2,128)} %copy.50), calls=%async_computation.2 | async-start | bytes 65536 | tf_op jit(solution)/shard_map/all_to_all | solution.py:103
  11.1 0.7 fusion.81
  12.3 3.0 %convolution_bitcast_fusion.1 = f32[1,2,8,32,128]{4,3,2,1,0:T(8,128)} fusion(f32[2,8,32,1024]{3,2,1,0:T(8,128)} %copy-done.1, f32[2,8,32]{2,1,0:T(8,128)S(1)} %get-tuple-element.24, pred[2,1024]{1,0:T(4,128)(4,1)} %bitcast.218, bf16[2,1024,128]{2,1,0:T(8,128)(2,1)S(1)} %copy-done.3), kind=kOutput, calls=%fused_computation.12 | convolution fusion | flops 136839168 | bytes 2887680 | tf_op jit(solution)/shard_map/pgnl,plh->pgnh/dot_general | solution.py:22
  15.3 0.7 constant_dynamic-slice_fusion.2
  16.1 0.8 constant_dynamic-slice_fusion
  17.9 0.7 copy.45
  18.6 4.2 %all-to-all-start.1 = ((f32[1,2,8,32]{2,1,0,3:T(2,128)}), f32[1,2,8,32]{2,1,0,3:T(2,128)S(1)}, u32[]{:S(2)}, u32[]{:S(2)}) async-start(f32[1,2,8,32]{2,1,0,3:T(2,128)} %copy.45), calls=%async_computation.1 | async-start | bytes 65536 | tf_op jit(solution)/shard_map/all_to_all | solution.py:102
  23.3 0.7 copy.56
  24.0 3.6 %all-to-all-done.1 = f32[1,2,8,32]{2,1,0,3:T(2,128)S(1)} async-done(((f32[1,2,8,32]{2,1,0,3:T(2,128)}), f32[1,2,8,32]{2,1,0,3:T(2,128)S(1)}, u32[]{:S(2)}, u32[]{:S(2)}) %all-to-all-start.1) | async-done | bytes 2080 | tf_op jit(solution)/shard_map/all_to_all | solution.py:102
  27.6 3.3 %all-to-all-start.4 = ((f32[1,2,8,32]{2,1,0,3:T(2,128)}), f32[1,2,8,32]{2,1,0,3:T(2,128)S(1)}, u32[]{:S(2)}, u32[]{:S(2)}) async-start(f32[1,2,8,32]{2,1,0,3:T(2,128)} %copy.56), calls=%async_computation.4 | async-start | bytes 65536 | tf_op jit(solution)/shard_map/all_to_all | solution.py:105
  31.2 0.9 copy.43
  32.0 0.8 copy.54
  32.9 0.7 copy.61
  33.6 0.6 dynamic-slice.3
  34.8 0.8 copy.51
  35.7 4.0 %all-to-all-start.5 = ((f32[1,2,8,32]{2,1,0,3:T(2,128)}), f32[1,2,8,32]{2,1,0,3:T(2,128)S(1)}, u32[]{:S(2)}, u32[]{:S(2)}) async-start(f32[1,2,8,32]{2,1,0,3:T(2,128)} %copy.61), calls=%async_computation.5 | async-start | bytes 65536 | tf_op jit(solution)/shard_map/all_to_all | solution.py:106
  39.8 4.8 %all-to-all-done.5 = f32[1,2,8,32]{2,1,0,3:T(2,128)S(1)} async-done(((f32[1,2,8,32]{2,1,0,3:T(2,128)}), f32[1,2,8,32]{2,1,0,3:T(2,128)S(1)}, u32[]{:S(2)}, u32[]{:S(2)}) %all-to-all-start.5) | async-done | bytes 2080 | tf_op jit(solution)/shard_map/all_to_all | solution.py:106
  44.6 3.4 %all-to-all-start = ((f32[1,2,8,32,128]{4,2,1,0,3:T(8,128)}), f32[1,2,8,32,128]{4,2,1,0,3:T(8,128)S(1)}, u32[]{:S(2)}, u32[]{:S(2)}) async-start(f32[1,2,8,32,128]{4,2,1,0,3:T(8,128)} %copy.43), calls=%async_computation | async-start | bytes 524288 | tf_op jit(solution)/shard_map/all_to_all | solution.py:104
  48.4 6.4 %all-to-all-done = f32[1,2,8,32,128]{4,2,1,0,3:T(8,128)S(1)} async-done(((f32[1,2,8,32,128]{4,2,1,0,3:T(8,128)}), f32[1,2,8,32,128]{4,2,1,0,3:T(8,128)S(1)}, u32[]{:S(2)}, u32[]{:S(2)}) %all-to-all-start) | async-done | bytes 262176 | tf_op jit(solution)/shard_map/all_to_all | solution.py:104
  54.8 3.4 %all-to-all-start.3 = ((f32[1,2,8,32,128]{4,2,1,0,3:T(8,128)}), f32[1,2,8,32,128]{4,2,1,0,3:T(8,128)S(1)}, u32[]{:S(2)}, u32[]{:S(2)}) async-start(f32[1,2,8,32,128]{4,2,1,0,3:T(8,128)} %copy.54), calls=%async_computation.3 | async-start | bytes 524288 | tf_op jit(solution)/shard_map/all_to_all | solution.py:107
  58.7 9.8 %all_gather.12 = bf16[2,32,1024]{2,0,1:T(2,128)(2,1)S(1)} all-gather(bf16[2,4,1024]{2,0,1:T(2,128)(2,1)S(1)} %copy.52), channel_id=1, replica_groups=mesh['seq'=8,'head'=4] {'seq'}, dimensions={1}, use_global_device_ids=true | all-gather | bytes 147456 | tf_op jit(solution)/shard_map/all_gather | solution.py:128
  68.6 16.5 %all_gather.13 = bf16[8,32,1024]{2,1,0:T(8,128)(2,1)S(1)} all-gather(bf16[2,32,1024]{2,1,0:T(8,128)(2,1)S(1)} %copy.53), channel_id=1, replica_groups=mesh['seq'=8,'head'=4] {'head'}, dimensions={0}, use_global_device_ids=true | all-gather | bytes 655360 | tf_op jit(solution)/shard_map/all_gather | solution.py:132
  85.5 9.2 %all_gather.14 = bf16[2,32,1024]{2,0,1:T(2,128)(2,1)S(1)} all-gather(bf16[2,4,1024]{2,0,1:T(2,128)(2,1)S(1)} %copy.63), channel_id=1, replica_groups=mesh['seq'=8,'head'=4] {'seq'}, dimensions={1}, use_global_device_ids=true | all-gather | bytes 147456 | tf_op jit(solution)/shard_map/all_gather | solution.py:129
  94.7 16.5 %all_gather.15 = bf16[8,32,1024]{2,1,0:T(8,128)(2,1)S(1)} all-gather(bf16[2,32,1024]{2,1,0:T(8,128)(2,1)S(1)} %copy.64), channel_id=1, replica_groups=mesh['seq'=8,'head'=4] {'head'}, dimensions={0}, use_global_device_ids=true | all-gather | bytes 655360 | tf_op jit(solution)/shard_map/all_gather | solution.py:133
  112.4 3.0 %fusion = f32[32,2,2048]{2,0,1:T(8,128)S(1)} fusion(bf16[1024,2048]{1,0:T(8,128)(2,1)} %param.15, bf16[32,2,8192]{2,0,1:T(8,128)(2,1)S(1)} %reshape.148, s32[]{:T(128)S(6)} %select_n.47), kind=kOutput, calls=%fused_computation | convolution fusion | flops 268435456 | bytes 4849668 | tf_op jit(solution)/shard_map/nrk,kd->nrd/dot_general | solution.py:143
  115.5 29.5 %all-reduce.2 = bf16[32,2,2048]{2,0,1:T(8,128)(2,1)S(1)} all-reduce(f32[32,2,2048]{2,0,1:T(8,128)S(1)} %fusion), channel_id=2, replica_groups=mesh['seq'=8,'head'=4] {'seq'}, use_global_device_ids=true, to_apply=%region_15.16.clone | all-reduce | flops 131072 | bytes 786432
  145.0 0.6 slice_bitcast_fusion
  (60 shorter events, 5.2 us)
Async XLA Ops:
  0.6 1.1 copy-start
  1.7 1.5 %copy-start.5 = (pred[1,2,8,128]{3,1,2,0:T(4,128)(4,1)}, pred[1,2,8,128]{3,1,2,0:T(4,128)(4,1)S(1)}, u32[]{:S(2)}) copy-start(pred[1,2,8,128]{3,1,2,0:T(4,128)(4,1)S(1)} %copy.92) | copy-start | bytes 6148
  1.7 9.4 %copy-start.2 = (bf16[2,2,8,32,128]{4,3,2,1,0:T(8,128)(2,1)S(1)}, bf16[2,2,8,32,128]{4,3,2,1,0:T(8,128)(2,1)}, u32[]{:S(2)}) copy-start(bf16[2,2,8,32,128]{4,3,2,1,0:T(8,128)(2,1)} %param.8) | copy-start | bytes 786436
  3.2 1.4 copy-start.1
  5.2 7.1 %copy-start.3 = (bf16[2,1024,128]{2,1,0:T(8,128)(2,1)S(1)}, bf16[2,1024,128]{2,1,0:T(8,128)(2,1)}, u32[]{:S(2)}) copy-start(bf16[2,1024,128]{2,1,0:T(8,128)(2,1)} %param.12) | copy-start | bytes 1572868
  5.9 12.7 %all-to-all-start.2 = ((f32[1,2,8,32]{2,1,0,3:T(2,128)}), f32[1,2,8,32]{2,1,0,3:T(2,128)}, u32[]{:S(2)}, u32[]{:S(2)}) async-start(f32[1,2,8,32]{2,1,0,3:T(2,128)} %copy.50), calls=%async_computation.2 | async-start | bytes 65536 | tf_op jit(solution)/shard_map/all_to_all | solution.py:103
  15.3 2.2 %copy-start.6 = (bf16[2,2,32,128]{3,2,1,0:T(8,128)(2,1)S(1)}, bf16[2,2,32,128]{3,2,1,0:T(8,128)(2,1)}, u32[]{:S(2)}) copy-start(bf16[2,2,32,128]{3,2,1,0:T(8,128)(2,1)} %param.9) | copy-start | bytes 98308
  16.1 1.8 %copy-start.7 = (pred[2,4,32]{2,1,0:T(4,128)(4,1)}, pred[2,4,32]{2,1,0:T(4,128)(4,1)S(1)}, u32[]{:S(2)}) copy-start(pred[2,4,32]{2,1,0:T(4,128)(4,1)S(1)} %fusion.67) | copy-start | bytes 772
  17.4 13.8 %copy-start.4 = (f32[1,2,8,32,128]{4,3,2,1,0:T(8,128)S(1)}, f32[1,2,8,32,128]{4,3,2,1,0:T(8,128)}, u32[]{:S(2)}) copy-start(f32[1,2,8,32,128]{4,3,2,1,0:T(8,128)} %convolution_bitcast_fusion.1) | copy-start | bytes 786436
  17.4 16.1 %copy-start.10 = (u32[32]{0:T(128)S(1)}, u32[32]{0:T(128)}, u32[]{:S(2)}) copy-start(u32[32]{0:T(128)} %constant.61) | copy-start | bytes 388
  17.9 13.1 %copy-start.8 = (pred[2,4,32]{2,1,0:T(4,128)(4,1)S(1)}, pred[2,4,32]{2,1,0:T(4,128)(4,1)}, u32[]{:S(2)}) copy-start(pred[2,4,32]{2,1,0:T(4,128)(4,1)} %copy-done.7) | copy-start | bytes 772
  18.6 9.0 %all-to-all-start.1 = ((f32[1,2,8,32]{2,1,0,3:T(2,128)}), f32[1,2,8,32]{2,1,0,3:T(2,128)S(1)}, u32[]{:S(2)}, u32[]{:S(2)}) async-start(f32[1,2,8,32]{2,1,0,3:T(2,128)} %copy.45), calls=%async_computation.1 | async-start | bytes 65536 | tf_op jit(solution)/shard_map/all_to_all | solution.py:102
  23.3 35.2 %copy-start.9 = (bf16[2,2,32,128]{3,2,1,0:T(8,128)(2,1)S(1)}, bf16[2,2,32,128]{3,2,1,0:T(8,128)(2,1)}, u32[]{:S(2)}) copy-start(bf16[2,2,32,128]{3,2,1,0:T(8,128)(2,1)} %param.10) | copy-start | bytes 98308
  27.6 8.1 %all-to-all-start.4 = ((f32[1,2,8,32]{2,1,0,3:T(2,128)}), f32[1,2,8,32]{2,1,0,3:T(2,128)S(1)}, u32[]{:S(2)}, u32[]{:S(2)}) async-start(f32[1,2,8,32]{2,1,0,3:T(2,128)} %copy.56), calls=%async_computation.4 | async-start | bytes 65536 | tf_op jit(solution)/shard_map/all_to_all | solution.py:105
  35.7 8.8 %all-to-all-start.5 = ((f32[1,2,8,32]{2,1,0,3:T(2,128)}), f32[1,2,8,32]{2,1,0,3:T(2,128)S(1)}, u32[]{:S(2)}, u32[]{:S(2)}) async-start(f32[1,2,8,32]{2,1,0,3:T(2,128)} %copy.61), calls=%async_computation.5 | async-start | bytes 65536 | tf_op jit(solution)/shard_map/all_to_all | solution.py:106
  44.6 10.3 %all-to-all-start = ((f32[1,2,8,32,128]{4,2,1,0,3:T(8,128)}), f32[1,2,8,32,128]{4,2,1,0,3:T(8,128)S(1)}, u32[]{:S(2)}, u32[]{:S(2)}) async-start(f32[1,2,8,32,128]{4,2,1,0,3:T(8,128)} %copy.43), calls=%async_computation | async-start | bytes 524288 | tf_op jit(solution)/shard_map/all_to_all | solution.py:104
  54.8 30.2 %all-to-all-start.3 = ((f32[1,2,8,32,128]{4,2,1,0,3:T(8,128)}), f32[1,2,8,32,128]{4,2,1,0,3:T(8,128)S(1)}, u32[]{:S(2)}, u32[]{:S(2)}) async-start(f32[1,2,8,32,128]{4,2,1,0,3:T(8,128)} %copy.54), calls=%async_computation.3 | async-start | bytes 524288 | tf_op jit(solution)/shard_map/all_to_all | solution.py:107
where the time goes:
time: 147 us; the launch traced here: 146 us
  blocking collectives  81.4 us (55%)
  starting transfers between devices  23.5 us (16%)
  waiting for transfers between devices  15 us (10%)
  local copies, waits for them, and re-layouts  11.7 us (8%)
  matrix products  9.38 us (6%)
  other arithmetic  2.98 us (2%)
  between operations  1.64 us (1%)
    unnamed x1, blocking collectives  29.5 us
    all_gather x1, blocking collectives, local(): lax.all_gather(verify_all, 'head', axis=0, tiled=True)  16.5 us
    all_gather x1, blocking collectives, local(): lax.all_gather(draft_all, 'head', axis=0, tiled=True)  16.5 us
    all_gather x1, blocking collectives, local(): lax.all_gather(finish(draft_cache, draft_tree), 'seq', axis=1, tiled=True)  9.83 us
    all_gather x1, blocking collectives, local(): lax.all_gather(finish(verify_cache, verify_tree), 'seq', axis=1, tiled=True)  9.17 us
    all_to_all x1, waiting for transfers between devices, local(): lax.all_to_all(draft_part[2][None], 'seq', split_axis=3, concat_axis=0, t...  6.41 us
    all_to_all x1, starting transfers between devices, local(): lax.all_to_all(draft_part[1][None], 'seq', split_axis=3, concat_axis=0, t...  5.2 us
    all_to_all x1, waiting for transfers between devices, local(): lax.all_to_all(verify_part[1][None], 'seq', split_axis=3, concat_axis=0,...  4.78 us
  transfers between devices with their start and end apart: 6, of which 4 were waited for; matrix products, arithmetic and copies ran while one was open for 9% of the time, Pallas kernels for 0%

commit v1 on v0

--- a/solution.py
+++ b/solution.py
@@ -2,9 +2,17 @@
 import jax.numpy as jnp
 from jax import lax
 from jax.sharding import PartitionSpec as P
+from jax.lax import all_to_all, axis_size
 
 KVH = 8
 BLOCK = 128
+
+
+def pack_cycles(view, named_axis):
+    m_next = jnp.split(view, axis_size(named_axis), axis=3)
+    w_next = all_to_all(jnp.stack(m_next), split_axis=0, concat_axis=0, axis_name=named_axis)
+    x_next = jnp.concatenate(w_next, axis=0)
+    return x_next
 
 
 def cache_partial(query_rows, key_rows, value_rows, chosen_mask, score_scale):
@@ -101,7 +109,7 @@
     arrived = (
         lax.all_to_all(draft_part[0][None], "seq", split_axis=3, concat_axis=0, tiled=True),
         lax.all_to_all(draft_part[1][None], "seq", split_axis=3, concat_axis=0, tiled=True),
-        lax.all_to_all(draft_part[2][None], "seq", split_axis=3, concat_axis=0, tiled=True),
+        pack_cycles(draft_part[2][None], "seq"),
         lax.all_to_all(verify_part[0][None], "seq", split_axis=3, concat_axis=0, tiled=True),
         lax.all_to_all(verify_part[1][None], "seq", split_axis=3, concat_axis=0, tiled=True),
         lax.all_to_all(verify_part[2][None], "seq", split_axis=3, concat_axis=0, tiled=True),

time: 147 us -> 151 us (1.027)
  local copies, waits for them, and re-layouts: 11.7 us -> 15.7 us
    unnamed x25 -> x26, local copies, waits for them, and re-layouts: 2.07 us -> 6.35 us
  transfers between devices with their start and end apart: 6 -> 6, of which waited for: 4 -> 4; matrix products, arithmetic and copies ran while one was open for 9% -> 12% of each run, Pallas kernels for 0% -> 0%
where the time goes in v1:
time: 151 us; the launch traced here: 150 us
  blocking collectives  81.4 us (54%)
  starting transfers between devices  22.9 us (15%)
  waiting for transfers between devices  15.8 us (10%)
  local copies, waits for them, and re-layouts  15.7 us (10%)
  matrix products  9.37 us (6%)
  other arithmetic  2.99 us (2%)
  between operations  1.62 us (1%)
    unnamed x1, blocking collectives  29.5 us
    all_gather x1, blocking collectives, local(): lax.all_gather(verify_all, 'head', axis=0, tiled=True)  16.5 us
    all_gather x1, blocking collectives, local(): lax.all_gather(draft_all, 'head', axis=0, tiled=True)  16.5 us
    all_gather x1, blocking collectives, local(): lax.all_gather(finish(draft_cache, draft_tree), 'seq', axis=1, tiled=True)  9.81 us
    all_gather x1, blocking collectives, local(): lax.all_gather(finish(verify_cache, verify_tree), 'seq', axis=1, tiled=True)  9.17 us
    all_to_all x1, waiting for transfers between devices, pack_cycles(): all_to_all(jnp.stack(m_next), split_axis=0, concat_axis=0, axis_name=name...  6.42 us
    unnamed x26, local copies, waits for them, and re-layouts  6.35 us
    all_to_all x1, starting transfers between devices, local(): lax.all_to_all(draft_part[1][None], 'seq', split_axis=3, concat_axis=0, t...  5.2 us
  transfers between devices with their start and end apart: 6, of which 4 were waited for; matrix products, arithmetic and copies ran while one was open for 12% of the time, Pallas kernels for 0%

profile of v1, /device:TPU:0, one launch (start us, length us, event | category | flops | bytes accessed | tf_op | source)
XLA Modules:
  0.0 149.8 jit_solution(18076260183175991145)
XLA Ops:
  0.7 0.9 compare_reduce_fusion
  1.7 1.5 fusion.2
  3.2 1.3 copy-done.1
  4.5 0.6 fusion.5
  5.2 0.7 copy.47
  5.9 5.2 %all-to-all-start.2 = ((f32[1,2,8,32]{2,1,0,3:T(2,128)}), f32[1,2,8,32]{2,1,0,3:T(2,128)}, u32[]{:S(2)}, u32[]{:S(2)}) async-start(f32[1,2,8,32]{2,1,0,3:T(2,128)} %copy.47), calls=%async_computation.2 | async-start | bytes 65536 | tf_op jit(solution)/shard_map/all_to_all | solution.py:111
  11.1 0.7 fusion.89
  12.3 2.2 %convolution_bitcast_fusion.1 = f32[1,2,8,32,128]{4,3,2,1,0:T(8,128)S(1)} fusion(f32[2,8,32,1024]{3,2,1,0:T(8,128)} %copy-done.1, f32[2,8,32]{2,1,0:T(8,128)S(1)} %get-tuple-element.24, pred[2,1024]{1,0:T(4,128)(4,1)} %bitcast.246, bf16[2,1024,128]{2,1,0:T(8,128)(2,1)S(1)} %copy-done.3), kind=kOutput, calls=%fused_computation.12 | convolution fusion | flops 136839168 | bytes 2887680 | tf_op jit(solution)/shard_map/pgnl,plh->pgnh/dot_general | solution.py:30
  19.5 0.7 constant_dynamic-slice_fusion.2
  20.3 0.8 constant_dynamic-slice_fusion
  21.8 0.9 fusion.90
  22.8 0.7 copy.42
  23.5 4.2 %all-to-all-start.1 = ((f32[1,2,8,32]{2,1,0,3:T(2,128)}), f32[1,2,8,32]{2,1,0,3:T(2,128)S(1)}, u32[]{:S(2)}, u32[]{:S(2)}) async-start(f32[1,2,8,32]{2,1,0,3:T(2,128)} %copy.42), calls=%async_computation.1 | async-start | bytes 65536 | tf_op jit(solution)/shard_map/all_to_all | solution.py:110
  28.2 0.7 copy.53
  28.9 3.6 %all-to-all-done.1 = f32[1,2,8,32]{2,1,0,3:T(2,128)S(1)} async-done(((f32[1,2,8,32]{2,1,0,3:T(2,128)}), f32[1,2,8,32]{2,1,0,3:T(2,128)S(1)}, u32[]{:S(2)}, u32[]{:S(2)}) %all-to-all-start.1) | async-done | bytes 2080 | tf_op jit(solution)/shard_map/all_to_all | solution.py:110
  32.5 3.3 %all-to-all-start.4 = ((f32[1,2,8,32]{2,1,0,3:T(2,128)}), f32[1,2,8,32]{2,1,0,3:T(2,128)S(1)}, u32[]{:S(2)}, u32[]{:S(2)}) async-start(f32[1,2,8,32]{2,1,0,3:T(2,128)} %copy.53), calls=%async_computation.4 | async-start | bytes 65536 | tf_op jit(solution)/shard_map/all_to_all | solution.py:113
  36.0 0.8 copy.51
  36.9 0.7 copy.58
  38.8 0.8 copy.48
  39.6 1.0 all-to-all-done.4
  40.6 3.3 %all-to-all-start.5 = ((f32[1,2,8,32]{2,1,0,3:T(2,128)}), f32[1,2,8,32]{2,1,0,3:T(2,128)S(1)}, u32[]{:S(2)}, u32[]{:S(2)}) async-start(f32[1,2,8,32]{2,1,0,3:T(2,128)} %copy.58), calls=%async_computation.5 | async-start | bytes 65536 | tf_op jit(solution)/shard_map/all_to_all | solution.py:114
  44.0 4.7 %all-to-all-done.5 = f32[1,2,8,32]{2,1,0,3:T(2,128)S(1)} async-done(((f32[1,2,8,32]{2,1,0,3:T(2,128)}), f32[1,2,8,32]{2,1,0,3:T(2,128)S(1)}, u32[]{:S(2)}, u32[]{:S(2)}) %all-to-all-start.5) | async-done | bytes 2080 | tf_op jit(solution)/shard_map/all_to_all | solution.py:114
  48.7 3.4 %all-to-all-start = ((f32[8,1,2,8,4,128]{5,4,3,2,1,0:T(4,128)}), f32[8,1,2,8,4,128]{5,4,3,2,1,0:T(4,128)S(1)}, u32[]{:S(2)}, u32[]{:S(2)}) async-start(f32[8,1,2,8,4,128]{5,4,3,2,1,0:T(4,128)} %fusion.37), calls=%async_computation | async-start | bytes 524288 | tf_op jit(solution)/shard_map/all_to_all | solution.py:13
  52.6 6.4 %all-to-all-done = f32[8,1,2,8,4,128]{5,4,3,2,1,0:T(4,128)S(1)} async-done(((f32[8,1,2,8,4,128]{5,4,3,2,1,0:T(4,128)}), f32[8,1,2,8,4,128]{5,4,3,2,1,0:T(4,128)S(1)}, u32[]{:S(2)}, u32[]{:S(2)}) %all-to-all-start) | async-done | bytes 262176 | tf_op jit(solution)/shard_map/all_to_all | solution.py:13
  59.0 3.4 %all-to-all-start.3 = ((f32[1,2,8,32,128]{4,2,1,0,3:T(8,128)}), f32[1,2,8,32,128]{4,2,1,0,3:T(8,128)S(1)}, u32[]{:S(2)}, u32[]{:S(2)}) async-start(f32[1,2,8,32,128]{4,2,1,0,3:T(8,128)} %copy.51), calls=%async_computation.3 | async-start | bytes 524288 | tf_op jit(solution)/shard_map/all_to_all | solution.py:115
  62.9 9.8 %all_gather.12 = bf16[2,32,1024]{2,0,1:T(2,128)(2,1)S(1)} all-gather(bf16[2,4,1024]{2,0,1:T(2,128)(2,1)S(1)} %copy.49), channel_id=1, replica_groups=mesh['seq'=8,'head'=4] {'seq'}, dimensions={1}, use_global_device_ids=true | all-gather | bytes 147456 | tf_op jit(solution)/shard_map/all_gather | solution.py:136
  72.7 16.5 %all_gather.13 = bf16[8,32,1024]{2,1,0:T(8,128)(2,1)S(1)} all-gather(bf16[2,32,1024]{2,1,0:T(8,128)(2,1)S(1)} %copy.50), channel_id=1, replica_groups=mesh['seq'=8,'head'=4] {'head'}, dimensions={0}, use_global_device_ids=true | all-gather | bytes 655360 | tf_op jit(solution)/shard_map/all_gather | solution.py:140
  89.7 9.2 %all_gather.14 = bf16[2,32,1024]{2,0,1:T(2,128)(2,1)S(1)} all-gather(bf16[2,4,1024]{2,0,1:T(2,128)(2,1)S(1)} %copy.60), channel_id=1, replica_groups=mesh['seq'=8,'head'=4] {'seq'}, dimensions={1}, use_global_device_ids=true | all-gather | bytes 147456 | tf_op jit(solution)/shard_map/all_gather | solution.py:137
  98.9 16.5 %all_gather.15 = bf16[8,32,1024]{2,1,0:T(8,128)(2,1)S(1)} all-gather(bf16[2,32,1024]{2,1,0:T(8,128)(2,1)S(1)} %copy.61), channel_id=1, replica_groups=mesh['seq'=8,'head'=4] {'head'}, dimensions={0}, use_global_device_ids=true | all-gather | bytes 655360 | tf_op jit(solution)/shard_map/all_gather | solution.py:141
  116.6 3.0 %fusion = f32[32,2,2048]{2,0,1:T(8,128)S(1)} fusion(bf16[1024,2048]{1,0:T(8,128)(2,1)} %param.15, bf16[32,2,8192]{2,0,1:T(8,128)(2,1)S(1)} %reshape.152, s32[]{:T(128)S(6)} %select_n.47), kind=kOutput, calls=%fused_computation | convolution fusion | flops 268435456 | bytes 4849668 | tf_op jit(solution)/shard_map/nrk,kd->nrd/dot_general | solution.py:151
  119.7 29.5 %all-reduce.2 = bf16[32,2,2048]{2,0,1:T(8,128)(2,1)S(1)} all-reduce(f32[32,2,2048]{2,0,1:T(8,128)S(1)} %fusion), channel_id=2, replica_groups=mesh['seq'=8,'head'=4] {'seq'}, use_global_device_ids=true, to_apply=%region_15.16.clone | all-reduce | flops 131072 | bytes 786432
  149.2 0.6 slice_bitcast_fusion.8
  (61 shorter events, 10.3 us)
Async XLA Ops:
  0.6 1.1 copy-start
  1.7 9.4 %copy-start.4 = (pred[1,2,8,128]{3,1,2,0:T(4,128)(4,1)}, pred[1,2,8,128]{3,1,2,0:T(4,128)(4,1)S(1)}, u32[]{:S(2)}) copy-start(pred[1,2,8,128]{3,1,2,0:T(4,128)(4,1)S(1)} %copy.88) | copy-start | bytes 6148
  1.7 9.4 %copy-start.2 = (bf16[2,2,8,32,128]{4,3,2,1,0:T(8,128)(2,1)S(1)}, bf16[2,2,8,32,128]{4,3,2,1,0:T(8,128)(2,1)}, u32[]{:S(2)}) copy-start(bf16[2,2,8,32,128]{4,3,2,1,0:T(8,128)(2,1)} %param.8) | copy-start | bytes 786436
  3.2 1.4 copy-start.1
  5.2 7.1 %copy-start.3 = (bf16[2,1024,128]{2,1,0:T(8,128)(2,1)S(1)}, bf16[2,1024,128]{2,1,0:T(8,128)(2,1)}, u32[]{:S(2)}) copy-start(bf16[2,1024,128]{2,1,0:T(8,128)(2,1)} %param.12) | copy-start | bytes 1572868
  5.9 17.6 %all-to-all-start.2 = ((f32[1,2,8,32]{2,1,0,3:T(2,128)}), f32[1,2,8,32]{2,1,0,3:T(2,128)}, u32[]{:S(2)}, u32[]{:S(2)}) async-start(f32[1,2,8,32]{2,1,0,3:T(2,128)} %copy.47), calls=%async_computation.2 | async-start | bytes 65536 | tf_op jit(solution)/shard_map/all_to_all | solution.py:111
  14.6 7.1 %copy-start.5 = (bf16[2,2,32,128]{3,2,1,0:T(8,128)(2,1)S(1)}, bf16[2,2,32,128]{3,2,1,0:T(8,128)(2,1)}, u32[]{:S(2)}) copy-start(bf16[2,2,32,128]{3,2,1,0:T(8,128)(2,1)} %param.9) | copy-start | bytes 98308
  21.6 16.0 %copy-start.7 = (u32[32]{0:T(128)S(1)}, u32[32]{0:T(128)}, u32[]{:S(2)}) copy-start(u32[32]{0:T(128)} %constant.61) | copy-start | bytes 388
  23.5 9.0 %all-to-all-start.1 = ((f32[1,2,8,32]{2,1,0,3:T(2,128)}), f32[1,2,8,32]{2,1,0,3:T(2,128)S(1)}, u32[]{:S(2)}, u32[]{:S(2)}) async-start(f32[1,2,8,32]{2,1,0,3:T(2,128)} %copy.42), calls=%async_computation.1 | async-start | bytes 65536 | tf_op jit(solution)/shard_map/all_to_all | solution.py:110
  27.7 35.0 %copy-start.6 = (bf16[2,2,32,128]{3,2,1,0:T(8,128)(2,1)S(1)}, bf16[2,2,32,128]{3,2,1,0:T(8,128)(2,1)}, u32[]{:S(2)}) copy-start(bf16[2,2,32,128]{3,2,1,0:T(8,128)(2,1)} %param.10) | copy-start | bytes 98308
  32.5 8.1 %all-to-all-start.4 = ((f32[1,2,8,32]{2,1,0,3:T(2,128)}), f32[1,2,8,32]{2,1,0,3:T(2,128)S(1)}, u32[]{:S(2)}, u32[]{:S(2)}) async-start(f32[1,2,8,32]{2,1,0,3:T(2,128)} %copy.53), calls=%async_computation.4 | async-start | bytes 65536 | tf_op jit(solution)/shard_map/all_to_all | solution.py:113
  40.6 8.1 %all-to-all-start.5 = ((f32[1,2,8,32]{2,1,0,3:T(2,128)}), f32[1,2,8,32]{2,1,0,3:T(2,128)S(1)}, u32[]{:S(2)}, u32[]{:S(2)}) async-start(f32[1,2,8,32]{2,1,0,3:T(2,128)} %copy.58), calls=%async_computation.5 | async-start | bytes 65536 | tf_op jit(solution)/shard_map/all_to_all | solution.py:114
  48.7 10.3 %all-to-all-start = ((f32[8,1,2,8,4,128]{5,4,3,2,1,0:T(4,128)}), f32[8,1,2,8,4,128]{5,4,3,2,1,0:T(4,128)S(1)}, u32[]{:S(2)}, u32[]{:S(2)}) async-start(f32[8,1,2,8,4,128]{5,4,3,2,1,0:T(4,128)} %fusion.37), calls=%async_computation | async-start | bytes 524288 | tf_op jit(solution)/shard_map/all_to_all | solution.py:13
  59.0 30.2 %all-to-all-start.3 = ((f32[1,2,8,32,128]{4,2,1,0,3:T(8,128)}), f32[1,2,8,32,128]{4,2,1,0,3:T(8,128)S(1)}, u32[]{:S(2)}, u32[]{:S(2)}) async-start(f32[1,2,8,32,128]{4,2,1,0,3:T(8,128)} %copy.51), calls=%async_computation.3 | async-start | bytes 524288 | tf_op jit(solution)/shard_map/all_to_all | solution.py:115
